TPU v7x, 32 devices: a whole 2x2x4 slice. The times are simulated.
32 devices in a mesh: groups: 2 (over y), tensor: 16 (over z, x, core).
Axes of the slice: x: 2, y: 2, z: 4, core: 2. Of those that a mesh axis runs over, the one named last changes fastest.
Arguments:
- normed_input: bfloat16 [16, 2, 8192], P('groups', None, 'tensor'), parts along dimension 0, may hold values from -6 to 6
- query_weight: bfloat16 [8192, 8192], P('tensor'), may hold values from -0.0625 to 0.0625
- query_gain: float32 [128], replicated, may hold values from 0.5 to 50
- image_cache: bfloat16 [32, 1601, 2048], P(('groups', 'tensor')), parts along dimension 0, may hold values from -18 to 18
- tile_count: int32 [16], P('groups'), parts along dimension 0, may hold values from 1 to 4, as said below
- image_first_slot: int32 [16], P('groups'), parts along dimension 0, may hold values from 0 to 15, as said below
- cross_tile_mask: int32 [16, 2, 4], P('groups'), parts along dimension 0, may hold values 0 or 1
- output_weight: bfloat16 [8192, 8192], P(None, 'tensor'), may hold values from -0.0625 to 0.0625
- output_gate: float32 [1], replicated, may hold values from 0.3 to 1.5
Outputs:
- cross_output: bfloat16 [16, 2, 8192], P('groups', None, 'tensor'), parts along dimension 0
There are 2 independent parts, one for each index of `groups`. A program takes and returns all parts, laid end to end along the dimension named above; an argument that names none is the same for every part. Nothing has to cross between parts.
Inputs may be any that keep to these rules, and one draw needn't show every extreme that they name: tile_count sums to 16; some row has 4 tiles. Row r's tiles are pool slots image_first_slot[r] to image_first_slot[r] + tile_count[r] - 1; the images fill all 16 slots, each slot belonging to exactly one row.
All inputs are finite; a program needn't handle non-finite values.
Results may differ from a plain program's by a relative error of at most 0.0077.
Values may be sent and summed in bfloat16 or wider, within the bound.
A program may use at most 64 MiB of HBM per device.

v0:
```python
import math
import jax
import jax.numpy as jnp
from jax import lax
from jax.sharding import PartitionSpec as P

EPSILON = 1e-05
NEGATIVE_FLOOR = -1e30


def membership(image_first_slot, tile_count, pool_slots):
    ends = image_first_slot + tile_count
    return (pool_slots[:, None] >= image_first_slot[None, :]) & (
        pool_slots[:, None] < ends[None, :]
    )


def active_status(member_flag, image_first_slot, cross_tile_mask, pool_slots):
    member_int = member_flag.astype(jnp.int32)
    tile_index = jnp.sum(member_int * (pool_slots[:, None] - image_first_slot[None, :]), axis=1)
    row_masks = jnp.sum(member_int[:, :, None, None] * cross_tile_mask[None], axis=1)
    positions = jnp.arange(cross_tile_mask.shape[2], dtype=jnp.int32)
    chosen = jnp.sum(
        jnp.where(positions[None, None, :] == tile_index[:, None, None], row_masks, 0), axis=2
    )
    return (tile_index[:, None] == 0) | (chosen == 1)


def tile_partial(query_rows, cache_tile, head_size):
    steps = query_rows.shape[0]
    kv_width = cache_tile.shape[1] // 2
    kv_heads = kv_width // head_size
    group = query_rows.shape[1] // kv_width
    grouped = query_rows.reshape(steps, kv_heads, group, head_size)
    keys = cache_tile[:, :kv_width].reshape(-1, kv_heads, head_size)
    values = cache_tile[:, kv_width:].reshape(-1, kv_heads, head_size)
    scores = jnp.einsum("skgd,tkd->skgt", grouped, keys, preferred_element_type=jnp.float32) * (
        1.0 / math.sqrt(head_size)
    )
    tops = jnp.max(scores, axis=3)
    weights = jnp.exp(scores - tops[..., None]).astype(jnp.bfloat16)
    totals = jnp.sum(weights.astype(jnp.float32), axis=3)
    mixed = jnp.einsum("skgt,tkd->skgd", weights, values, preferred_element_type=jnp.float32)
    return (tops.reshape(steps, -1), totals.reshape(steps, -1), mixed.reshape(steps, -1))


def finish(numer_pairs, denom_pairs, head_size):
    pairs = numer_pairs.shape[0]
    heads = denom_pairs.shape[1]
    shaped = numer_pairs.reshape(pairs, heads, head_size) / denom_pairs[..., None]
    return shaped.astype(jnp.bfloat16).reshape(pairs, heads * head_size)


def body(
    normed_input,
    query_weight,
    query_gain,
    image_cache,
    tile_count,
    image_first_slot,
    cross_tile_mask,
    output_weight,
    output_gate,
):
    rows, steps, local_width = normed_input.shape
    head_size = query_gain.shape[0]
    heads = query_weight.shape[1] // head_size
    slot_count = image_cache.shape[0]
    flattened = normed_input.reshape(rows * steps, local_width)
    query = lax.psum_scatter(
        jnp.dot(flattened, query_weight, preferred_element_type=jnp.float32),
        "tensor",
        scatter_dimension=0,
        tiled=True,
    )
    shaped = query.reshape(slot_count, heads, head_size)
    normed = (
        shaped * lax.rsqrt(jnp.mean(shaped * shaped, axis=2, keepdims=True) + EPSILON) * query_gain
    )
    normed = normed.astype(jnp.bfloat16).reshape(slot_count, heads * head_size)
    all_queries = lax.all_gather(normed, "tensor", axis=0, tiled=True)
    target_device = lax.axis_index("tensor")
    pool_slots = target_device * slot_count + jnp.arange(slot_count, dtype=jnp.int32)
    member_flag = membership(image_first_slot, tile_count, pool_slots)
    active_entry = active_status(member_flag, image_first_slot, cross_tile_mask, pool_slots)
    by_row = all_queries.reshape(rows, steps * heads * head_size)
    selected = jnp.dot(member_flag.astype(jnp.bfloat16), by_row, preferred_element_type=jnp.float32)
    selected = selected.astype(jnp.bfloat16).reshape(slot_count, steps, heads * head_size)

    def slot_term(operands):
        return tile_partial(operands[0], operands[1], head_size)

    tops, totals, mixed = lax.map(slot_term, (selected, image_cache))
    masked = jnp.where(active_entry[:, :, None], tops, NEGATIVE_FLOOR)
    pair_index = target_device * slot_count + jnp.arange(slot_count, dtype=jnp.int32)
    pair_row = pair_index // steps
    pair_step = pair_index % steps
    gathered_tops, gathered_totals, gathered_mixed = (
        lax.all_gather(masked, "tensor", axis=0, tiled=True),
        lax.all_gather(totals, "tensor", axis=0, tiled=True),
        lax.all_gather(mixed, "tensor", axis=0, tiled=True),
    )
    all_slots = gathered_tops.shape[0]
    every_slot = jnp.arange(all_slots, dtype=jnp.int32)
    full_member = membership(image_first_slot, tile_count, every_slot)
    slot_pick = full_member[:, pair_row]
    step_pick = jnp.arange(steps, dtype=jnp.int32)[None, :] == pair_step[:, None]
    chosen = slot_pick[:, :, None] & step_pick[None, :, :]
    spread = jnp.where(chosen[..., None], gathered_tops[:, None, :, :], NEGATIVE_FLOOR)
    pair_max = jnp.max(spread, axis=(0, 2))
    weights = jnp.where(chosen[..., None], jnp.exp(spread - pair_max[None, :, None, :]), 0.0)
    denom_pairs = jnp.sum(weights * gathered_totals[:, None, :, :], axis=(0, 2))
    mixed_heads = gathered_mixed.reshape(all_slots, steps, heads, head_size)
    numer_pairs = jnp.einsum(
        "spth,sthd->phd", weights, mixed_heads, precision=lax.Precision.HIGHEST
    )
    numer_pairs = numer_pairs.reshape(slot_count, heads * head_size)
    attended = finish(numer_pairs, denom_pairs, head_size)
    projected = jnp.dot(
        lax.all_gather(attended, "tensor", axis=0, tiled=True),
        output_weight,
        preferred_element_type=jnp.float32,
    )
    result = jnp.tanh(output_gate[0]) * projected
    return result.astype(jnp.bfloat16).reshape(rows, steps, -1)


def solution(mesh):
    return jax.shard_map(
        body,
        mesh=mesh,
        in_specs=(
            P("groups", None, "tensor"),
            P("tensor", None),
            P(),
            P(("groups", "tensor"), None, None),
            P("groups"),
            P("groups"),
            P("groups", None, None),
            P(None, "tensor"),
            P(),
        ),
        out_specs=P("groups", None, "tensor"),
        check_vma=False,
    )
```

profile of v0, /device:TPU:0, one launch (start us, length us, event | category | flops | bytes accessed | tf_op | source)
XLA Modules:
  0.0 217.2 jit_solution(3710583259249691234)
XLA Ops:
  6.5 0.0 all-reduce.3.cloned.1.call-start
  6.5 0.7 reshape.264
  7.3 5.4 %fusion.27 = f32[16,8192]{1,0:T(8,128)} fusion(bf16[16,512]{1,0:T(8,128)(2,1)S(1)} %reshape.264, bf16[512,8192]{1,0:T(8,128)(2,1)} %param.10), kind=kOutput, calls=%fused_computation.45 | convolution fusion | flops 134217728 | bytes 8929280 | tf_op jit(solution)/shard_map/dot_general | solution.py:71
  12.6 0.0 all-reduce.3.cloned.1.call-update
  12.7 0.0 all-gather.4.cloned.1.call-start
  12.7 3.7 %fusion.25 = (bf16[1601,1024]{1,0:T(8,128)(2,1)S(1)}, bf16[1601,1024]{1,0:T(8,128)(2,1)S(1)}) fusion(bf16[1601,2048]{1,0:T(8,128)(2,1)} %bitcast.51), kind=kLoop, calls=%fused_computation.43 | loop fusion | bytes 13115392 | tf_op jit(solution)/shard_map/while/body/eval_jaxpr/slice | solution.py:36
  16.4 0.9 copy.38
  17.3 0.3 slice_bitcast_fusion.1
  17.6 0.9 copy.39
  18.4 0.0 copy-start.6
  18.4 0.0 copy-start.2
  18.4 0.0 copy-start.5
  18.5 0.0 copy-start.4
  18.5 1.8 slice_bitcast_fusion
  20.3 0.0 copy-done.6
  20.3 0.6 dynamic-slice.4
  20.9 0.0 copy-done.2
  20.9 0.0 copy-done.5
  20.9 0.6 select_reduce_fusion.1
  21.5 84.8 %all-reduce.3.cloned.1.call-done = f32[16,8192]{1,0:T(8,128)} async-done(((f32[16,8192]{1,0:T(8,128)}), f32[16,8192]{1,0:T(8,128)}) %all-reduce.3.cloned.1.call-update) | async-done | bytes 524304
  106.3 1.6 dynamic-slice_multiply_fusion
  107.9 0.1 reduce_sum.55
  108.0 0.0 copy-done.4
  108.0 0.1 mul.75
  108.1 1.7 convert_bitcast_fusion
  109.8 23.6 %all-gather = bf16[16,1,8192]{2,1,0:T(2,128)(2,1)} all-gather(bf16[1,1,8192]{2,1,0:T(2,128)(2,1)S(1)} %convert_bitcast_fusion), channel_id=1, replica_groups=mesh['groups'=2,'tensor'=16] {'tensor'}, dimensions={0}, use_global_device_ids=true | all-gather | bytes 278528 | tf_op jit(solution)/shard_map/all_gather | solution.py:81
  133.4 3.2 %reduce.12 = bf16[16,8192]{1,0:T(8,128)(2,1)} reduce(bf16[16,1,8192]{2,1,0:T(2,128)(2,1)} %all-gather, bf16[]{:T(256)} %constant.103), dimensions={1}, to_apply=%all-gather.reduce_sub_computation | reduce | bytes 524290 | tf_op jit(solution)/shard_map/all_gather | solution.py:81
  136.6 1.1 reshape.265
  137.7 0.0 copy-start
  137.7 0.2 fusion.21
  137.9 1.1 fusion.26
  139.0 0.0 copy-start.1
  139.0 0.0 copy-start.3
  139.0 0.6 copy-done
  139.6 1.2 fusion.10
  140.8 0.0 copy-done.1
  140.8 0.7 broadcast_in_dim.87
  141.5 0.0 all-gather.4.cloned.1.call-update
  141.5 0.6 iota_compare_fusion.2
  143.4 0.1 fusion.20
  143.4 0.0 copy-done.3
  143.5 0.2 multiply_reduce_fusion.1
  143.6 0.1 select_reduce_fusion
  143.7 0.1 broadcast_and_fusion
  143.8 1.4 convert_reduce_fusion
  145.3 0.1 broadcast_in_dim.97
  145.3 0.1 broadcast_in_dim.93
  145.4 17.5 %all_gather.18 = f32[16,2,64]{2,1,0:T(2,128)S(1)} all-gather(f32[1,2,64]{2,1,0:T(2,128)S(1)} %broadcast_in_dim.97), channel_id=1, replica_groups=mesh['groups'=2,'tensor'=16] {'tensor'}, dimensions={0}, use_global_device_ids=true | all-gather | bytes 8704 | tf_op jit(solution)/shard_map/all_gather | solution.py:100
  162.9 0.1 broadcast_select_fusion.1
  163.0 19.0 %all_gather.17 = f32[16,2,64]{2,1,0:T(2,128)S(1)} all-gather(f32[1,2,64]{2,1,0:T(2,128)S(1)} %broadcast_select_fusion.1), channel_id=1, replica_groups=mesh['groups'=2,'tensor'=16] {'tensor'}, dimensions={0}, use_global_device_ids=true | all-gather | bytes 8704 | tf_op jit(solution)/shard_map/all_gather | solution.py:99
  181.9 0.1 fusion.19
  182.0 0.1 multiply_reduce_fusion
  182.1 0.1 copy.31
  182.2 0.0 all-gather.4.cloned.1.call-done
  182.3 2.1 reshape.269
  184.4 1.7 fusion.14
  186.1 0.1 divide_convert_fusion
  186.2 18.9 %all-gather.1 = bf16[16,1,8192]{2,1,0:T(2,128)(2,1)S(1)} all-gather(bf16[1,1,8192]{2,1,0:T(2,128)(2,1)S(1)} %reshape.298), channel_id=1, replica_groups=mesh['groups'=2,'tensor'=16] {'tensor'}, dimensions={0}, use_global_device_ids=true | all-gather | bytes 278528 | tf_op jit(solution)/shard_map/all_gather | solution.py:120
  205.1 4.6 %fusion.13 = bf16[16,512]{1,0:T(8,128)(2,1)S(1)} fusion(bf16[8192,512]{1,0:T(8,128)(2,1)} %param.16, bf16[16,1,8192]{2,1,0:T(2,128)(2,1)S(1)} %all-gather.1, f32[]{:T(128)} %bitcast), kind=kOutput, calls=%fused_computation.10 | convolution fusion | flops 134234112 | bytes 8667140 | tf_op jit(solution)/shard_map/dot_general | solution.py:119
  209.7 0.6 reshape.271
  (11 shorter events, 0.1 us)
Async XLA Ops:
  6.5 99.7 %all-reduce.3.cloned.1.call-start = ((), (), s32[]{:S(2)}) async-start(), calls=%async_computation.1 | async-start | bytes 1048576
  12.7 169.6 %all-gather.4.cloned.1.call-start = ((), (), s32[]{:S(2)}) async-start(), calls=%async_computation | async-start | bytes 1114112 | tf_op jit(solution)/shard_map/all_gather | solution.py:101
  18.4 1.9 copy-start.6
  18.4 2.4 %copy-start.2 = (s32[8]{0:T(128)S(1)}, s32[8]{0:T(128)}, u32[]{:S(2)}) copy-start(s32[8]{0:T(128)} %param.14) | copy-start | bytes 100
  18.4 2.4 %copy-start.5 = (s32[8]{0:T(128)S(1)}, s32[8]{0:T(128)}, u32[]{:S(2)}) copy-start(s32[8]{0:T(128)} %param.13) | copy-start | bytes 100
  18.5 89.6 %copy-start.4 = (f32[128]{0:T(128)S(1)}, f32[128]{0:T(128)}, u32[]{:S(2)}) copy-start(f32[128]{0:T(128)} %param.11) | copy-start | bytes 1540
  137.7 1.9 copy-start
  139.0 1.8 copy-start.1
  139.0 4.4 %copy-start.3 = (s32[8,2,4]{0,2,1:T(4,128)S(1)}, s32[8,2,4]{0,2,1:T(4,128)}, u32[]{:S(2)}) copy-start(s32[8,2,4]{0,2,1:T(4,128)} %param.15) | copy-start | bytes 772
Sparse Core Ops, SparseCore 0:
  12.8 93.4 all-reduce.2
  141.6 35.1 all-gather.3
where the time goes:
time: 218 us; the launch traced here: 217 us
  waiting for transfers between devices  84.8 us (39%)
  blocking collectives  78.9 us (36%)
  between operations  14.9 us (7%)
  local copies, waits for them, and re-layouts  14.2 us (7%)
  matrix products  14.2 us (7%)
  other arithmetic  10.1 us (5%)
    unnamed x3, waiting for transfers between devices  84.8 us
    all_gather x1, blocking collectives, body(): all_queries = lax.all_gather(normed, 'tensor', axis=0, tiled=True)  23.6 us
    all_gather x1, blocking collectives, body(): lax.all_gather(masked, 'tensor', axis=0, tiled=True)  19 us
    all_gather x1, blocking collectives, body(): lax.all_gather(attended, 'tensor', axis=0, tiled=True)  18.9 us
    all_gather x1, blocking collectives, body(): lax.all_gather(totals, 'tensor', axis=0, tiled=True)  17.5 us
    dot_general x1, matrix products, body(): jnp.dot(flattened, query_weight, preferred_element_type=jnp.float32)  5.38 us
    dot_general x1, matrix products, body(): jnp.dot(lax.all_gather(attended, 'tensor', axis=0, tiled=True), output_we...  4.62 us
  transfers between devices with their start and end apart: 2, of which 1 were waited for; matrix products, arithmetic and copies ran while one was open for 5% of the time, Pallas kernels for 0%

commit v1 on v0

--- a/solution.py
+++ b/solution.py
@@ -6,6 +6,19 @@
 
 EPSILON = 1e-05
 NEGATIVE_FLOOR = -1e30
+
+
+def ring_gather(x, axis, dim):
+    ways = lax.axis_size(axis)
+    up = [(d, (d + 1) % ways) for d in range(ways)]
+    down = [(d, (d - 1) % ways) for d in range(ways)]
+    earlier, later = ([x], [x])
+    for _ in range(ways // 2):
+        earlier.append(lax.ppermute(earlier[-1], axis, up))
+    for _ in range((ways - 1) // 2):
+        later.append(lax.ppermute(later[-1], axis, down))
+    line = jnp.concatenate([*earlier[::-1], *later[1:]], axis=dim)
+    return jnp.roll(line, (lax.axis_index(axis) - ways // 2) * x.shape[dim], axis=dim)
 
 
 def membership(image_first_slot, tile_count, pool_slots):
@@ -96,7 +109,7 @@
     pair_row = pair_index // steps
     pair_step = pair_index % steps
     gathered_tops, gathered_totals, gathered_mixed = (
-        lax.all_gather(masked, "tensor", axis=0, tiled=True),
+        ring_gather(masked, "tensor", 0),
         lax.all_gather(totals, "tensor", axis=0, tiled=True),
         lax.all_gather(mixed, "tensor", axis=0, tiled=True),
     )

time: 218 us -> 275 us (1.26)
  waiting for transfers between devices: 84.8 us -> 125 us
  starting transfers between devices: 0.04 us -> 28.4 us
  blocking collectives: 78.9 us -> 62.4 us
  matrix products: 14.2 us -> 18.1 us
    all_gather x1, waiting for transfers between devices: 0.02 us -> 32.6 us  [body(): lax.all_gather(mixed, 'tensor', axis=0, tiled=True)]
    ppermute x0 -> x15, starting transfers between devices: none -> 28.4 us  [the longest x7 28 us: ring_gather(): later.append(lax.ppermute(later[-1], axis, down))]
    all_gather x1 -> x0, blocking collectives: 19 us -> none  [body(): lax.all_gather(masked, 'tensor', axis=0, tiled=True)]
    ppermute x0 -> x15, waiting for transfers between devices: none -> 10.4 us  [the longest x8 7.54 us: ring_gather(): earlier.append(lax.ppermute(earlier[-1], axis, up))]
    unnamed x3, waiting for transfers between devices: 84.8 us -> 81.6 us
  transfers between devices with their start and end apart: 2 -> 17, of which waited for: 1 -> 10; matrix products, arithmetic and copies ran while one was open for 5% -> 6% of each run, Pallas kernels for 0% -> 0%
where the time goes in v1:
time: 275 us; the launch traced here: 274 us
  waiting for transfers between devices  125 us (45%)
  blocking collectives  62.4 us (23%)
  starting transfers between devices  28.4 us (10%)
  matrix products  18.1 us (7%)
  local copies, waits for them, and re-layouts  15 us (5%)
  between operations  15 us (5%)
  other arithmetic  11 us (4%)
    unnamed x3, waiting for transfers between devices  81.6 us
    all_gather x1, waiting for transfers between devices, body(): lax.all_gather(mixed, 'tensor', axis=0, tiled=True)  32.6 us
    ppermute x7, starting transfers between devices, ring_gather(): later.append(lax.ppermute(later[-1], axis, down))  28 us
    all_gather x1, blocking collectives, body(): all_queries = lax.all_gather(normed, 'tensor', axis=0, tiled=True)  23.6 us
    all_gather x1, blocking collectives, body(): lax.all_gather(attended, 'tensor', axis=0, tiled=True)  20.8 us
    all_gather x1, blocking collectives, body(): lax.all_gather(totals, 'tensor', axis=0, tiled=True)  18 us
    ppermute x8, waiting for transfers between devices, ring_gather(): earlier.append(lax.ppermute(earlier[-1], axis, up))  7.54 us
  transfers between devices with their start and end apart: 17, of which 10 were waited for; matrix products, arithmetic and copies ran while one was open for 6% of the time, Pallas kernels for 0%

profile of v1, /device:TPU:0, one launch (start us, length us, event | category | flops | bytes accessed | tf_op | source)
XLA Modules:
  0.0 274.5 jit_solution(336167784993820770)
XLA Ops:
  6.5 0.7 reshape.264
  7.3 5.4 %fusion.27 = f32[16,8192]{1,0:T(8,128)} fusion(bf16[16,512]{1,0:T(8,128)(2,1)S(1)} %reshape.264, bf16[512,8192]{1,0:T(8,128)(2,1)} %param.10), kind=kOutput, calls=%fused_computation.77 | convolution fusion | flops 134217728 | bytes 8929280 | tf_op jit(solution)/shard_map/dot_general | solution.py:84
  12.7 0.0 all-gather.4.cloned.1.call-start
  12.7 3.7 %fusion.25 = (bf16[1601,1024]{1,0:T(8,128)(2,1)S(1)}, bf16[1601,1024]{1,0:T(8,128)(2,1)S(1)}) fusion(bf16[1601,2048]{1,0:T(8,128)(2,1)} %bitcast.51), kind=kLoop, calls=%fused_computation.75 | loop fusion | bytes 13115392 | tf_op jit(solution)/shard_map/while/body/eval_jaxpr/slice | solution.py:49
  16.4 0.9 copy.38
  17.3 1.8 slice_bitcast_fusion.1
  19.1 0.6 select_reduce_fusion.1
  19.8 0.6 iota_compare_fusion.2
  21.1 0.9 copy.39
  22.0 0.3 slice_bitcast_fusion
  22.2 0.4 copy-done.2
  22.6 0.1 multiply_reduce_fusion.1
  22.8 0.1 select_reduce_fusion
  22.9 0.5 iota_compare_fusion.3
  23.4 0.7 dynamic-slice.4
  24.1 0.6 fusion.20
  24.7 81.5 %all-reduce.3.cloned.1.call-done = f32[16,8192]{1,0:T(8,128)} async-done(((f32[16,8192]{1,0:T(8,128)}), f32[16,8192]{1,0:T(8,128)}) %all-reduce.3.cloned.1.call-update) | async-done | bytes 524304
  106.3 1.7 dynamic-slice_multiply_fusion
  107.9 0.1 reduce_sum.55
  108.1 0.1 mul.75
  108.2 1.7 convert_bitcast_fusion
  109.9 23.6 %all-gather = bf16[16,1,8192]{2,1,0:T(2,128)(2,1)} all-gather(bf16[1,1,8192]{2,1,0:T(2,128)(2,1)S(1)} %convert_bitcast_fusion), channel_id=1, replica_groups=mesh['groups'=2,'tensor'=16] {'tensor'}, dimensions={0}, use_global_device_ids=true | all-gather | bytes 278528 | tf_op jit(solution)/shard_map/all_gather | solution.py:94
  133.5 3.3 %reduce.12 = bf16[16,8192]{1,0:T(8,128)(2,1)} reduce(bf16[16,1,8192]{2,1,0:T(2,128)(2,1)} %all-gather, bf16[]{:T(256)} %constant.127), dimensions={1}, to_apply=%all-gather.reduce_sub_computation | reduce | bytes 524290 | tf_op jit(solution)/shard_map/all_gather | solution.py:94
  136.7 1.1 reshape.265
  137.8 0.2 fusion.21
  138.0 3.9 %fusion.26 = (f32[2,8,8]{2,0,1:T(2,128)S(1)}, f32[2,8,8,1601]{3,2,0,1:T(8,128)}) fusion(bf16[1601,8,128,1]{2,1,0,3:T(8,128)(2,1)} %slice_bitcast_fusion.1, bf16[2,8,8,128]{3,2,1,0:T(8,128)(2,1)S(1)} %bitcast.53), kind=kOutput, calls=%fused_computation.76 | convolution fusion | flops 52871296 | bytes 4131840 | tf_op jit(solution)/shard_map/while/body/eval_jaxpr/skgd,tkd->skgt/dot_general | solution.py:50
  141.9 0.1 broadcast_in_dim.93
  142.0 0.1 broadcast_select_fusion
  142.0 0.4 collective-permute-start
  142.4 5.3 %collective-permute-done = f32[1,2,64]{2,1,0:T(2,128)S(1)} collective-permute-done((f32[1,2,64]{2,1,0:T(2,128)S(1)}, f32[1,2,64]{2,1,0:T(2,128)S(1)}, u32[]{:S(2)}, u32[]{:S(2)}) %collective-permute-start) | collective-permute-done | bytes 544 | tf_op jit(solution)/shard_map/ppermute | solution.py:17
  147.7 0.7 dynamic-slice_bitcast_fusion
  148.4 4.4 %collective-permute-start.8 = (f32[1,2,64]{2,1,0:T(2,128)S(1)}, f32[1,2,64]{2,1,0:T(2,128)S(1)}, u32[]{:S(2)}, u32[]{:S(2)}) collective-permute-start(f32[1,2,64]{2,1,0:T(2,128)S(1)} %broadcast_select_fusion), channel_id=1, source_target_pairs={{0,15},{1,0},{2,1},{3,2},{4,3},{5,4},{6,5},{7,6},{8,7},{9,8},{10,9... | collective-permute-start | bytes 1544 | tf_op jit(solution)/shard_map/ppermute | solution.py:19
  152.9 0.6 collective-permute-done.1
  153.4 0.7 broadcast_and_fusion
  154.1 0.0 collective-permute-done.8
  154.2 4.4 %collective-permute-start.9 = (f32[1,2,64]{2,1,0:T(2,128)S(1)}, f32[1,2,64]{2,1,0:T(2,128)S(1)}, u32[]{:S(2)}, u32[]{:S(2)}) collective-permute-start(f32[1,2,64]{2,1,0:T(2,128)S(1)} %collective-permute-done.8), channel_id=1, source_target_pairs={{0,15},{1,0},{2,1},{3,2},{4,3},{5,4},{6,5},{7,6},{8,7},{9,8},{10,9... | collective-permute-start | bytes 1544 | tf_op jit(solution)/shard_map/ppermute | solution.py:19
  158.6 0.6 collective-permute-done.2
  159.1 0.7 collective-permute-done.9
  159.9 4.4 %collective-permute-start.10 = (f32[1,2,64]{2,1,0:T(2,128)S(1)}, f32[1,2,64]{2,1,0:T(2,128)S(1)}, u32[]{:S(2)}, u32[]{:S(2)}) collective-permute-start(f32[1,2,64]{2,1,0:T(2,128)S(1)} %collective-permute-done.9), channel_id=1, source_target_pairs={{0,15},{1,0},{2,1},{3,2},{4,3},{5,4},{6,5},{7,6},{8,7},{9,8},{10,9... | collective-permute-start | bytes 1544 | tf_op jit(solution)/shard_map/ppermute | solution.py:19
  164.3 0.6 collective-permute-done.3
  165.6 4.5 %collective-permute-start.11 = (f32[1,2,64]{2,1,0:T(2,128)S(1)}, f32[1,2,64]{2,1,0:T(2,128)S(1)}, u32[]{:S(2)}, u32[]{:S(2)}) collective-permute-start(f32[1,2,64]{2,1,0:T(2,128)S(1)} %collective-permute-done.10), channel_id=1, source_target_pairs={{0,15},{1,0},{2,1},{3,2},{4,3},{5,4},{6,5},{7,6},{8,7},{9,8},{10,9... | collective-permute-start | bytes 1544 | tf_op jit(solution)/shard_map/ppermute | solution.py:19
  170.0 0.5 collective-permute-done.4
  170.5 2.3 fusion.10
  172.9 4.5 %collective-permute-start.12 = (f32[1,2,64]{2,1,0:T(2,128)S(1)}, f32[1,2,64]{2,1,0:T(2,128)S(1)}, u32[]{:S(2)}, u32[]{:S(2)}) collective-permute-start(f32[1,2,64]{2,1,0:T(2,128)S(1)} %collective-permute-done.11), channel_id=1, source_target_pairs={{0,15},{1,0},{2,1},{3,2},{4,3},{5,4},{6,5},{7,6},{8,7},{9,8},{10,9... | collective-permute-start | bytes 1544 | tf_op jit(solution)/shard_map/ppermute | solution.py:19
  177.4 0.3 convert_reduce_fusion
  177.6 0.1 broadcast_in_dim.97
  177.7 0.9 collective-permute-done.12
  178.6 4.4 %collective-permute-start.13 = (f32[1,2,64]{2,1,0:T(2,128)S(1)}, f32[1,2,64]{2,1,0:T(2,128)S(1)}, u32[]{:S(2)}, u32[]{:S(2)}) collective-permute-start(f32[1,2,64]{2,1,0:T(2,128)S(1)} %collective-permute-done.12), channel_id=1, source_target_pairs={{0,15},{1,0},{2,1},{3,2},{4,3},{5,4},{6,5},{7,6},{8,7},{9,8},{10,9... | collective-permute-start | bytes 1544 | tf_op jit(solution)/shard_map/ppermute | solution.py:19
  183.0 18.0 %all_gather.14 = f32[16,2,64]{2,1,0:T(2,128)S(1)} all-gather(f32[1,2,64]{2,1,0:T(2,128)S(1)} %broadcast_in_dim.97), channel_id=1, replica_groups=mesh['groups'=2,'tensor'=16] {'tensor'}, dimensions={0}, use_global_device_ids=true | all-gather | bytes 8704 | tf_op jit(solution)/shard_map/all_gather | solution.py:113
  201.1 0.7 broadcast_in_dim.87
  201.8 1.4 collective-permute-start.14
  203.3 0.1 constant_dynamic-update-slice_fusion.23
  203.4 1.1 collective-permute-done.14
  204.6 0.1 constant_dynamic-update-slice_fusion.7
  204.7 0.1 fusion.19
  204.8 0.1 multiply_reduce_fusion
  204.9 0.1 copy.31
  205.0 32.6 %all-gather.4.cloned.1.call-done = f32[16,2,8192]{2,1,0:T(2,128)} async-done(((f32[1,2,8192]{2,1,0:T(2,128)}), f32[16,2,8192]{2,1,0:T(2,128)}) %all-gather.4.cloned.1.call-update) | async-done | bytes 1048592 | tf_op jit(solution)/shard_map/all_gather | solution.py:114
  237.7 2.1 reshape.269
  239.8 1.7 fusion.14
  241.5 0.1 divide_convert_fusion
  241.6 20.8 %all-gather.1 = bf16[16,1,8192]{2,1,0:T(2,128)(2,1)S(1)} all-gather(bf16[1,1,8192]{2,1,0:T(2,128)(2,1)S(1)} %reshape.298), channel_id=1, replica_groups=mesh['groups'=2,'tensor'=16] {'tensor'}, dimensions={0}, use_global_device_ids=true | all-gather | bytes 278528 | tf_op jit(solution)/shard_map/all_gather | solution.py:133
  262.4 4.6 %fusion.13 = bf16[16,512]{1,0:T(8,128)(2,1)S(1)} fusion(bf16[8192,512]{1,0:T(8,128)(2,1)} %param.16, bf16[16,1,8192]{2,1,0:T(2,128)(2,1)S(1)} %all-gather.1, f32[]{:T(128)} %bitcast), kind=kOutput, calls=%fused_computation.10 | convolution fusion | flops 134234112 | bytes 8667140 | tf_op jit(solution)/shard_map/dot_general | solution.py:132
  267.0 0.6 reshape.271
  (66 shorter events, 0.4 us)
Async XLA Ops:
  6.5 99.7 %all-reduce.3.cloned.1.call-start = ((), (), s32[]{:S(2)}) async-start(), calls=%async_computation.1 | async-start | bytes 1048576
  12.7 225.0 %all-gather.4.cloned.1.call-start = ((), (), s32[]{:S(2)}) async-start(), calls=%async_computation | async-start | bytes 1114112 | tf_op jit(solution)/shard_map/all_gather | solution.py:114
  17.3 1.8 copy-start.1
  17.3 1.8 copy-start.4
  21.9 0.7 copy-start.2
  21.9 1.5 copy-start.5
  22.0 86.1 %copy-start.3 = (f32[128]{0:T(128)S(1)}, f32[128]{0:T(128)}, u32[]{:S(2)}) copy-start(f32[128]{0:T(128)} %param.11) | copy-start | bytes 1540
  142.0 5.7 %collective-permute-start = (f32[1,2,64]{2,1,0:T(2,128)S(1)}, f32[1,2,64]{2,1,0:T(2,128)S(1)}, u32[]{:S(2)}, u32[]{:S(2)}) collective-permute-start(f32[1,2,64]{2,1,0:T(2,128)S(1)} %broadcast_select_fusion), channel_id=1, source_target_pairs={{0,1},{1,2},{2,3},{3,4},{4,5},{5,6},{6,7},{7,8},{8,9},{9,10},{10,1... | collective-permute-start | bytes 1544 | tf_op jit(solution)/shard_map/ppermute | solution.py:17
  147.7 5.7 %collective-permute-start.1 = (f32[1,2,64]{2,1,0:T(2,128)S(1)}, f32[1,2,64]{2,1,0:T(2,128)S(1)}, u32[]{:S(2)}, u32[]{:S(2)}) collective-permute-start(f32[1,2,64]{2,1,0:T(2,128)S(1)} %collective-permute-done), channel_id=1, source_target_pairs={{0,1},{1,2},{2,3},{3,4},{4,5},{5,6},{6,7},{7,8},{8,9},{9,10},{10,1... | collective-permute-start | bytes 1544 | tf_op jit(solution)/shard_map/ppermute | solution.py:17
  148.4 5.7 %collective-permute-start.8 = (f32[1,2,64]{2,1,0:T(2,128)S(1)}, f32[1,2,64]{2,1,0:T(2,128)S(1)}, u32[]{:S(2)}, u32[]{:S(2)}) collective-permute-start(f32[1,2,64]{2,1,0:T(2,128)S(1)} %broadcast_select_fusion), channel_id=1, source_target_pairs={{0,15},{1,0},{2,1},{3,2},{4,3},{5,4},{6,5},{7,6},{8,7},{9,8},{10,9... | collective-permute-start | bytes 1544 | tf_op jit(solution)/shard_map/ppermute | solution.py:19
  153.4 5.7 %collective-permute-start.2 = (f32[1,2,64]{2,1,0:T(2,128)S(1)}, f32[1,2,64]{2,1,0:T(2,128)S(1)}, u32[]{:S(2)}, u32[]{:S(2)}) collective-permute-start(f32[1,2,64]{2,1,0:T(2,128)S(1)} %collective-permute-done.1), channel_id=1, source_target_pairs={{0,1},{1,2},{2,3},{3,4},{4,5},{5,6},{6,7},{7,8},{8,9},{9,10},{10,1... | collective-permute-start | bytes 1544 | tf_op jit(solution)/shard_map/ppermute | solution.py:17
  154.2 5.7 %collective-permute-start.9 = (f32[1,2,64]{2,1,0:T(2,128)S(1)}, f32[1,2,64]{2,1,0:T(2,128)S(1)}, u32[]{:S(2)}, u32[]{:S(2)}) collective-permute-start(f32[1,2,64]{2,1,0:T(2,128)S(1)} %collective-permute-done.8), channel_id=1, source_target_pairs={{0,15},{1,0},{2,1},{3,2},{4,3},{5,4},{6,5},{7,6},{8,7},{9,8},{10,9... | collective-permute-start | bytes 1544 | tf_op jit(solution)/shard_map/ppermute | solution.py:19
  159.1 5.7 %collective-permute-start.3 = (f32[1,2,64]{2,1,0:T(2,128)S(1)}, f32[1,2,64]{2,1,0:T(2,128)S(1)}, u32[]{:S(2)}, u32[]{:S(2)}) collective-permute-start(f32[1,2,64]{2,1,0:T(2,128)S(1)} %collective-permute-done.2), channel_id=1, source_target_pairs={{0,1},{1,2},{2,3},{3,4},{4,5},{5,6},{6,7},{7,8},{8,9},{9,10},{10,1... | collective-permute-start | bytes 1544 | tf_op jit(solution)/shard_map/ppermute | solution.py:17
  159.9 5.7 %collective-permute-start.10 = (f32[1,2,64]{2,1,0:T(2,128)S(1)}, f32[1,2,64]{2,1,0:T(2,128)S(1)}, u32[]{:S(2)}, u32[]{:S(2)}) collective-permute-start(f32[1,2,64]{2,1,0:T(2,128)S(1)} %collective-permute-done.9), channel_id=1, source_target_pairs={{0,15},{1,0},{2,1},{3,2},{4,3},{5,4},{6,5},{7,6},{8,7},{9,8},{10,9... | collective-permute-start | bytes 1544 | tf_op jit(solution)/shard_map/ppermute | solution.py:19
  164.8 5.7 %collective-permute-start.4 = (f32[1,2,64]{2,1,0:T(2,128)S(1)}, f32[1,2,64]{2,1,0:T(2,128)S(1)}, u32[]{:S(2)}, u32[]{:S(2)}) collective-permute-start(f32[1,2,64]{2,1,0:T(2,128)S(1)} %collective-permute-done.3), channel_id=1, source_target_pairs={{0,1},{1,2},{2,3},{3,4},{4,5},{5,6},{6,7},{7,8},{8,9},{9,10},{10,1... | collective-permute-start | bytes 1544 | tf_op jit(solution)/shard_map/ppermute | solution.py:17
  165.5 11.8 %copy-start = (f32[2,8,8,1601]{3,2,0,1:T(8,128)S(1)}, f32[2,8,8,1601]{3,2,0,1:T(8,128)}, u32[]{:S(2)}) copy-start(f32[2,8,8,1601]{3,2,0,1:T(8,128)} %get-tuple-element.41) | copy-start | bytes 2459140
  165.6 7.3 %collective-permute-start.11 = (f32[1,2,64]{2,1,0:T(2,128)S(1)}, f32[1,2,64]{2,1,0:T(2,128)S(1)}, u32[]{:S(2)}, u32[]{:S(2)}) collective-permute-start(f32[1,2,64]{2,1,0:T(2,128)S(1)} %collective-permute-done.10), channel_id=1, source_target_pairs={{0,15},{1,0},{2,1},{3,2},{4,3},{5,4},{6,5},{7,6},{8,7},{9,8},{10,9... | collective-permute-start | bytes 1544 | tf_op jit(solution)/shard_map/ppermute | solution.py:19
  170.5 6.8 %collective-permute-start.5 = (f32[1,2,64]{2,1,0:T(2,128)S(1)}, f32[1,2,64]{2,1,0:T(2,128)S(1)}, u32[]{:S(2)}, u32[]{:S(2)}) collective-permute-start(f32[1,2,64]{2,1,0:T(2,128)S(1)} %collective-permute-done.4), channel_id=1, source_target_pairs={{0,1},{1,2},{2,3},{3,4},{4,5},{5,6},{6,7},{7,8},{8,9},{9,10},{10,1... | collective-permute-start | bytes 1544 | tf_op jit(solution)/shard_map/ppermute | solution.py:17
  172.9 5.8 %collective-permute-start.12 = (f32[1,2,64]{2,1,0:T(2,128)S(1)}, f32[1,2,64]{2,1,0:T(2,128)S(1)}, u32[]{:S(2)}, u32[]{:S(2)}) collective-permute-start(f32[1,2,64]{2,1,0:T(2,128)S(1)} %collective-permute-done.11), channel_id=1, source_target_pairs={{0,15},{1,0},{2,1},{3,2},{4,3},{5,4},{6,5},{7,6},{8,7},{9,8},{10,9... | collective-permute-start | bytes 1544 | tf_op jit(solution)/shard_map/ppermute | solution.py:19
  177.3 5.7 %collective-permute-start.6 = (f32[1,2,64]{2,1,0:T(2,128)S(1)}, f32[1,2,64]{2,1,0:T(2,128)S(1)}, u32[]{:S(2)}, u32[]{:S(2)}) collective-permute-start(f32[1,2,64]{2,1,0:T(2,128)S(1)} %collective-permute-done.5), channel_id=1, source_target_pairs={{0,1},{1,2},{2,3},{3,4},{4,5},{5,6},{6,7},{7,8},{8,9},{9,10},{10,1... | collective-permute-start | bytes 1544 | tf_op jit(solution)/shard_map/ppermute | solution.py:17
  178.6 23.1 %collective-permute-start.13 = (f32[1,2,64]{2,1,0:T(2,128)S(1)}, f32[1,2,64]{2,1,0:T(2,128)S(1)}, u32[]{:S(2)}, u32[]{:S(2)}) collective-permute-start(f32[1,2,64]{2,1,0:T(2,128)S(1)} %collective-permute-done.12), channel_id=1, source_target_pairs={{0,15},{1,0},{2,1},{3,2},{4,3},{5,4},{6,5},{7,6},{8,7},{9,8},{10,9... | collective-permute-start | bytes 1544 | tf_op jit(solution)/shard_map/ppermute | solution.py:19
  183.0 20.1 %collective-permute-start.7 = (f32[1,2,64]{2,1,0:T(2,128)S(1)}, f32[1,2,64]{2,1,0:T(2,128)S(1)}, u32[]{:S(2)}, u32[]{:S(2)}) collective-permute-start(f32[1,2,64]{2,1,0:T(2,128)S(1)} %collective-permute-done.6), channel_id=1, source_target_pairs={{0,1},{1,2},{2,3},{3,4},{4,5},{5,6},{6,7},{7,8},{8,9},{9,10},{10,1... | collective-permute-start | bytes 1544 | tf_op jit(solution)/shard_map/ppermute | solution.py:17
  201.8 2.7 collective-permute-start.14
Sparse Core Ops, SparseCore 0:
  12.8 93.4 all-reduce.2
  201.9 35.7 all-gather.3
